TPU v7x, 256 devices: a whole 4x4x8 slice. The times are simulated.
256 devices in a mesh: ctx: 32 (over y, z), tp: 8 (over x, core).
Axes of the slice: x: 4, y: 4, z: 8, core: 2. Of those that a mesh axis runs over, the one named last changes fastest.
Arguments:
- ssm_inputs: bfloat16 [8192, 8192], P('ctx', 'tp'), may hold values from -4 to 4
- state_maps: bfloat16 [8192, 8, 256], P('ctx', 'tp'), may hold values from -4 to 4
- ssm_gates: bfloat16 [8192, 8192], P('ctx', 'tp'), may hold values from -4 to 4
- time_steps: float32 [128, 8192], P('tp', 'ctx'), may hold values from -5 to 512
- log_rates: float32 [128], P('tp'), may hold values from -12 to 1
- skip_gain: float32 [128], P('tp'), may hold values from 0.5 to 2
- conv_inputs: bfloat16 [4, 8192], P(None, 'tp'), may hold values from -3 to 3
- conv_maps: bfloat16 [4, 8, 256], P(None, 'tp'), may hold values from -3 to 3
- norm_gain: float32 [8192], P('tp'), may hold values from 0.1 to 1.9
- out_weight: bfloat16 [8192, 4096], P('tp'), may hold values from -0.0625 to 0.0625
- queries: bfloat16 [8192, 8192], P('ctx', 'tp'), may hold values from -5 to 5
- attention_keys: bfloat16 [8192, 1024], P('ctx', 'tp'), may hold values from -5 to 5
- values: bfloat16 [8192, 1024], P('ctx', 'tp'), may hold values from -4 to 4
Outputs:
- ssm_out: bfloat16 [8192, 4096], P(('ctx', 'tp'))
- attn_out: bfloat16 [8192, 8192], P('ctx', 'tp')
All inputs are finite; a program needn't handle non-finite values.
Results may differ from a plain program's by a relative error of at most 0.03.
Values may be sent and summed in bfloat16 or wider, within the bound.
No kernel may reach another device: no remote copies, remote signals or barrier semaphores. Data moves between devices by JAX's collectives and lax.ppermute only.
A program may use at most 128 MiB of HBM per device.

v0:
```python
import jax
import jax.numpy as jnp
from jax import lax
from jax.sharding import PartitionSpec as P

QUERY_HEADS = 64
KEY_VALUE_HEADS = 8
HEAD_SIZE = 128


def passed_along(shard, axis, by):
    size = lax.axis_size(axis)
    pairs = [(i, i + by) for i in range(size) if 0 <= i + by < size]
    return lax.ppermute(shard, axis, pairs)


def prefix_2(shard, axis, join, neutral):
    place = lax.axis_index(axis)
    gathered = jax.tree.map(
        lambda a, kind: lax.all_gather(a.astype(kind), axis), shard, (jnp.bfloat16, jnp.bfloat16)
    )
    state = jax.tree.map(lambda a, e: jnp.zeros_like(a) + jnp.asarray(e, a.dtype), shard, neutral)

    def one(step, state):
        return join(
            state,
            jax.tree.map(
                lambda a, own: lax.dynamic_index_in_dim(a, step, 0, False).astype(own.dtype),
                gathered,
                shard,
            ),
        )

    return lax.fori_loop(0, place, one, state)


def conv_silu(extended, conv_taps, tok_rows):
    summed = jnp.zeros((tok_rows,) + extended.shape[1:], jnp.float32)
    for tap_index in range(conv_taps.shape[0]):
        summed = summed + conv_taps[tap_index].astype(jnp.float32) * extended[
            tap_index : tap_index + tok_rows
        ].astype(jnp.float32)
    return jax.nn.silu(summed).astype(jnp.bfloat16)


def per_device(
    ssm_inputs,
    state_maps,
    ssm_gates,
    time_steps,
    log_rates,
    skip_gain,
    conv_inputs,
    conv_maps,
    norm_gain,
    out_weight,
    queries,
    attention_keys,
    values,
):
    tok_rows = ssm_inputs.shape[0]
    tap_count = conv_inputs.shape[0]
    groups_here = state_maps.shape[1]
    state_size = state_maps.shape[2] // 2
    heads_here = log_rates.shape[0]
    per_group = heads_here // groups_here
    head_dim = ssm_inputs.shape[1] // heads_here
    my_index = lax.axis_index("ctx")
    lead_inputs, lead_maps = passed_along(
        (ssm_inputs[tok_rows - tap_count + 1 :], state_maps[tok_rows - tap_count + 1 :]), "ctx", 1
    )
    mixed_inputs = conv_silu(
        jnp.concatenate([lead_inputs, ssm_inputs], axis=0), conv_inputs, tok_rows
    )
    mixed_maps = conv_silu(jnp.concatenate([lead_maps, state_maps], axis=0), conv_maps, tok_rows)
    input_heads = mixed_inputs.reshape(tok_rows, groups_here, per_group, head_dim)
    b_maps = mixed_maps[:, :, :state_size]
    c_maps = mixed_maps[:, :, state_size:]
    step_sizes = jax.nn.softplus(time_steps).reshape(groups_here, per_group, tok_rows)
    decline_rate = -jnp.exp(log_rates).reshape(groups_here, per_group)
    running_log = jnp.cumsum(step_sizes * decline_rate[:, :, None], axis=2)
    map_products = jnp.einsum("tgn,sgn->gts", c_maps, b_maps, preferred_element_type=jnp.float32)
    token_location = jnp.arange(tok_rows)
    causal = token_location[:, None] >= token_location[None, :]
    log_gap = running_log[:, :, :, None] - running_log[:, :, None, :]
    decay_table = jnp.where(causal, jnp.exp(jnp.minimum(log_gap, 0.0)), 0.0)
    mixer = (map_products[:, None] * decay_table * step_sizes[:, :, None, :]).astype(jnp.bfloat16)
    inner_part = jnp.einsum(
        "gjts,sgjp->tgjp", mixer, input_heads, preferred_element_type=jnp.float32
    )
    inputs_float = input_heads.astype(jnp.float32)
    tail_weight = jnp.exp(running_log[:, :, -1:] - running_log) * step_sizes
    weighted = (jnp.transpose(tail_weight, (2, 0, 1))[..., None] * inputs_float).astype(
        jnp.bfloat16
    )
    block_state = jnp.einsum("sgjp,sgn->gjpn", weighted, b_maps, preferred_element_type=jnp.float32)
    block_decay = running_log[:, :, -1]

    def combine(earlier, later):
        return (earlier[0] + later[0], jnp.exp(later[0])[:, :, None, None] * earlier[1] + later[1])

    prefix = prefix_2(
        (block_decay, block_state),
        "ctx",
        combine,
        (jnp.zeros_like(block_decay), jnp.zeros_like(block_state)),
    )
    entering = prefix[1]
    carried = jnp.einsum(
        "tgn,gjpn->tgjp", c_maps.astype(jnp.float32), entering, precision=lax.Precision.HIGHEST
    )
    outside = jnp.transpose(jnp.exp(running_log), (2, 0, 1))[..., None] * carried
    ssm_output = (
        inner_part
        + outside
        + skip_gain.reshape(groups_here, per_group)[None, :, :, None] * inputs_float
    )
    channel_count = per_group * head_dim
    gated = ssm_output.reshape(tok_rows, groups_here, channel_count) * jax.nn.silu(
        ssm_gates.reshape(tok_rows, groups_here, channel_count).astype(jnp.float32)
    )
    mean_square = jnp.mean(gated * gated, axis=2, keepdims=True)
    normed = (
        (gated * lax.rsqrt(mean_square + 1e-05)).reshape(tok_rows, groups_here * channel_count)
        * norm_gain
    ).astype(jnp.bfloat16)
    ssm_out = lax.psum_scatter(
        jnp.dot(normed, out_weight, preferred_element_type=jnp.float32).astype(jnp.bfloat16),
        "tp",
        scatter_dimension=0,
        tiled=True,
    )
    kv_heads = attention_keys.shape[1] // HEAD_SIZE
    shared_heads = QUERY_HEADS // KEY_VALUE_HEADS
    score_scale = HEAD_SIZE ** (-0.5)
    query_pos = my_index * tok_rows + token_location
    query_heads = queries.reshape(tok_rows, kv_heads, shared_heads, HEAD_SIZE)
    block_rows = tok_rows // 4
    first_key = jnp.int32(0)
    key_block = lax.all_gather(attention_keys, "ctx", axis=0, tiled=True)
    value_block = lax.all_gather(values, "ctx", axis=0, tiled=True)
    key_count = key_block.shape[0]
    key_head_rows = key_block.reshape(key_count, kv_heads, HEAD_SIZE)
    value_head_rows = value_block.reshape(key_count, kv_heads, HEAD_SIZE)
    key_pos = jnp.arange(key_count)
    peaks = jnp.full((kv_heads, shared_heads, tok_rows), -1e30, jnp.float32)
    totals = jnp.zeros((kv_heads, shared_heads, tok_rows), jnp.float32)
    sums = jnp.zeros((kv_heads, shared_heads, tok_rows, HEAD_SIZE), jnp.float32)
    new_parts = []
    for current_block_index in range(4):
        row_lower = current_block_index * block_rows
        row_upper = row_lower + block_rows
        query_tile_block = query_heads[row_lower:row_upper]
        block_pos = query_pos[row_lower:row_upper]
        old_state = (
            peaks[:, :, row_lower:row_upper],
            totals[:, :, row_lower:row_upper],
            sums[:, :, row_lower:row_upper],
        )

        def update(old_part, query_tile_block=query_tile_block, block_pos=block_pos):
            old_peak, old_total, old_sum = old_part
            scores = (
                jnp.einsum(
                    "bgrd,kgd->grbk",
                    query_tile_block,
                    key_head_rows,
                    preferred_element_type=jnp.float32,
                )
                * score_scale
            )
            allowed = key_pos[None, :] <= block_pos[:, None]
            scores = jnp.where(allowed, scores, -1e30)
            new_peak = jnp.maximum(old_peak, jnp.max(scores, axis=3))
            weights = jnp.where(allowed, jnp.exp(scores - new_peak[..., None]), 0.0)
            new_total = jnp.sum(weights, axis=3)
            new_sum = jnp.einsum(
                "grbk,kgd->grbd",
                weights.astype(jnp.bfloat16),
                value_head_rows,
                preferred_element_type=jnp.float32,
            )
            return (new_peak, new_total, new_sum)

        def unchanged(old_part):
            return old_part

        new_parts.append(
            lax.cond(block_pos[block_rows - 1] >= first_key, update, unchanged, old_state)
        )
    peaks, totals, sums = tuple(
        (
            jnp.concatenate([block_part[member] for block_part in new_parts], axis=2)
            for member in range(3)
        )
    )
    attended = sums / totals[..., None]
    attn_out = (
        jnp.transpose(attended, (2, 0, 1, 3))
        .reshape(tok_rows, kv_heads * shared_heads * HEAD_SIZE)
        .astype(jnp.bfloat16)
    )
    return (ssm_out, attn_out)


def solution(mesh):
    placed = (
        P("ctx", "tp"),
        P("ctx", "tp", None),
        P("ctx", "tp"),
        P("tp", "ctx"),
        P("tp"),
        P("tp"),
        P(None, "tp"),
        P(None, "tp", None),
        P("tp"),
        P("tp", None),
        P("ctx", "tp"),
        P("ctx", "tp"),
        P("ctx", "tp"),
    )
    return jax.shard_map(
        per_device,
        mesh=mesh,
        in_specs=placed,
        out_specs=(P(("ctx", "tp"), None), P("ctx", "tp")),
        check_vma=False,
    )
```

profile of v0, /device:TPU:4, one launch (start us, length us, event | category | flops | bytes accessed | tf_op | source)
XLA Modules:
  0.0 351.8 jit_solution(560110108480496360)
XLA Ops:
  8.2 3.8 %collective-permute-start = (bf16[3,1024]{0,1:T(8,128)(2,1)S(1)}, bf16[3,1024]{0,1:T(8,128)(2,1)S(1)}, u32[]{:S(2)}, u32[]{:S(2)}) collective-permute-start(bf16[3,1024]{0,1:T(8,128)(2,1)S(1)} %copy.76), channel_id=1, source_target_pairs={{0,8},{8,16},{16,24},{24,32},{32,40},{40,48},{48,56},{56,64},{64,7... | collective-permute-start | bytes 18440 | tf_op jit(solution)/shard_map/ppermute | solution.py:14
  12.7 3.8 %collective-permute-start.1 = (bf16[3,1,256]{2,0,1:T(4,128)(2,1)S(1)}, bf16[3,1,256]{2,0,1:T(4,128)(2,1)S(1)}, u32[]{:S(2)}, u32[]{:S(2)}) collective-permute-start(bf16[3,1,256]{2,0,1:T(4,128)(2,1)S(1)} %slice.125), channel_id=1, source_target_pairs={{0,8},{8,16},{16,24},{24,32},{32,40},{40,48},{48,56},{56,64},{64,7... | collective-permute-start | bytes 4616 | tf_op jit(solution)/shard_map/ppermute | solution.py:14
  24.3 1.5 fusion.96
  28.3 40.3 %all-gather = bf16[32,16,1]{1,2,0:T(2,128)(2,1)S(1)} all-gather(bf16[1,16,1]{1,2,0:T(2,128)(2,1)S(1)} %slice.213), channel_id=2, replica_groups=mesh['ctx'=32,'tp'=8] {'ctx'}, dimensions={0}, use_global_device_ids=true | all-gather | bytes 1056 | tf_op jit(solution)/shard_map/all_gather | solution.py:20
  71.8 54.2 %all-gather.10.cloned.1.call-done = bf16[512,64,128]{2,1,0:T(8,128)(2,1)} async-done(((bf16[16,64,128]{2,1,0:T(8,128)(2,1)}), bf16[512,64,128]{2,1,0:T(8,128)(2,1)}) %all-gather.10.cloned.1.call-update) | async-done | bytes 8388624 | tf_op jit(solution)/shard_map/all_gather | solution.py:20
  127.0 7.2 %convolution_convert_fusion = bf16[256,4096]{1,0:T(8,128)(2,1)} fusion(bf16[1024,4096]{1,0:T(8,128)(2,1)} %param.32, f32[256,1024]{0,1:T(8,128)S(1)} %get-tuple-element.171, f32[1024]{0:T(1024)S(1)} %copy-done, f32[256]{0:T(256)S(1)} %add_rsqrt_fusion), kind=kOutput, calls=%fused_computation.82 | convolution fusion | flops 2149318656 | bytes 11539456 | tf_op jit(solution)/shard_map/dot_general | solution.py:128
  137.2 66.5 %all-gather.6.cloned.1.call-done = bf16[8192,128]{1,0:T(8,128)(2,1)} async-done(((bf16[256,128]{1,0:T(8,128)(2,1)}), bf16[8192,128]{1,0:T(8,128)(2,1)}) %all-gather.6.cloned.1.call-update) | async-done | bytes 2097168 | tf_op jit(solution)/shard_map/all_gather | solution.py:140
  203.7 77.8 %all-gather.8.cloned.1.call-done = bf16[8192,128]{1,0:T(8,128)(2,1)} async-done(((bf16[256,128]{1,0:T(8,128)(2,1)}), bf16[8192,128]{1,0:T(8,128)(2,1)}) %all-gather.8.cloned.1.call-update) | async-done | bytes 2097168 | tf_op jit(solution)/shard_map/all_gather | solution.py:141
  281.5 15.4 %conditional.4 = (f32[1,8,64]{2,1,0:T(8,128)S(1)}, f32[1,8,64,128]{3,2,1,0:T(8,128)S(1)}) conditional(s32[]{:T(128)} %bitcast.73, () %tuple.48, (s32[8192]{0:T(1024)S(1)}, s32[256]{0:T(256)S(1)}, bf16[8192,1,128]{2,0,1:T(8,128)(2,1)}, bf16[256,1024]{1,0:T(8,128)(2,1)}, bf16[8192,1,128]{2,0,1:T(8,128)(2,1)}) %tuple.109), branch_computations={%region_6.7_spmd, %region_7.10_spmd} | conditional | flops 2202533376 | bytes 65450796 | solution.py:189
  281.8 4.8 %fusion = (f32[8,64]{1,0:T(8,128)S(1)}, f32[8192,64,8]{0,1,2:T(8,128)S(1)}) fusion(pred[64,8192]{1,0:T(8,128)(4,1)S(1)} %broadcast_compare_fusion, bf16[8192,1,128]{2,0,1:T(8,128)(2,1)} %get-tuple-element.97, bf16[256,1024]{1,0:T(8,128)(2,1)} %get-tuple-element.98), kind=kOutput, calls=%fused_computation.4 | convolution fusion | flops 1086324224 | bytes 19531776 | tf_op jit(solution)/shard_map/cond/branch_1_fun/bgrd,kgd->grbk/dot_general | solution.py:164
  286.7 4.7 %fusion.10 = f32[1,8,64,128]{3,2,1,0:T(8,128)S(1)} fusion(bf16[8192,1,128]{2,0,1:T(8,128)(2,1)S(1)} %copy-done.2, f32[8192,64,8]{0,1,2:T(8,128)S(1)} %get-tuple-element.179, f32[8,64]{1,0:T(8,128)S(1)} %broadcast_maximum_fusion, pred[64,8192]{1,0:T(8,128)(4,1)S(1)} %broadcast_compare_fusion), kind=kOutput, calls=%fused_computation.13 | convolution fusion | flops 1094713344 | bytes 19662848 | tf_op jit(solution)/shard_map/cond/branch_1_fun/grbk,kgd->grbd/dot_general | solution.py:177
  291.4 5.5 %fusion.2 = f32[8,64]{1,0:T(8,128)S(1)} fusion(f32[8192,64,8]{0,1,2:T(8,128)S(1)} %get-tuple-element.179, f32[8,64]{1,0:T(8,128)S(1)} %broadcast_maximum_fusion, pred[64,8192]{1,0:T(8,128)(4,1)S(1)} %broadcast_compare_fusion), kind=kLoop, calls=%fused_computation.6 | loop fusion | flops 20971008 | bytes 17305600 | tf_op jit(solution)/shard_map/cond/branch_1_fun/reduce_sum | solution.py:176
  296.9 15.5 %conditional.5 = (f32[1,8,64]{2,1,0:T(8,128)S(1)}, f32[1,8,64,128]{3,2,1,0:T(8,128)S(1)}) conditional(s32[]{:T(128)} %bitcast.76, () %tuple.50, (s32[8192]{0:T(1024)S(1)}, s32[256]{0:T(256)S(1)}, bf16[8192,1,128]{2,0,1:T(8,128)(2,1)}, bf16[256,1024]{1,0:T(8,128)(2,1)}, bf16[8192,1,128]{2,0,1:T(8,128)(2,1)}) %tuple.110), branch_computations={%region_10.11_spmd, %region_11.14_spmd} | conditional | flops 2202533376 | bytes 65450796 | solution.py:189
  297.3 4.9 %fusion.20 = (f32[8,64]{1,0:T(8,128)S(1)}, f32[8192,64,8]{0,1,2:T(8,128)S(1)}) fusion(pred[64,8192]{1,0:T(8,128)(4,1)S(1)} %broadcast_compare_fusion.1, bf16[8192,1,128]{2,0,1:T(8,128)(2,1)} %get-tuple-element.102, bf16[256,1024]{1,0:T(8,128)(2,1)} %get-tuple-element.103), kind=kOutput, calls=%fused_computation.24 | convolution fusion | flops 1086324224 | bytes 19531776 | tf_op jit(solution)/shard_map/cond/branch_1_fun/bgrd,kgd->grbk/dot_general | solution.py:164
  302.2 4.7 %fusion.30 = f32[1,8,64,128]{3,2,1,0:T(8,128)S(1)} fusion(bf16[8192,1,128]{2,0,1:T(8,128)(2,1)S(1)} %copy-done.3, f32[8192,64,8]{0,1,2:T(8,128)S(1)} %get-tuple-element.181, f32[8,64]{1,0:T(8,128)S(1)} %broadcast_maximum_fusion.1, pred[64,8192]{1,0:T(8,128)(4,1)S(1)} %broadcast_compare_fusion.1), kind=kOutput, calls=%fused_computation.33 | convolution fusion | flops 1094713344 | bytes 19662848 | tf_op jit(solution)/shard_map/cond/branch_1_fun/grbk,kgd->grbd/dot_general | solution.py:177
  306.9 5.5 %fusion.22 = f32[8,64]{1,0:T(8,128)S(1)} fusion(f32[8192,64,8]{0,1,2:T(8,128)S(1)} %get-tuple-element.181, f32[8,64]{1,0:T(8,128)S(1)} %broadcast_maximum_fusion.1, pred[64,8192]{1,0:T(8,128)(4,1)S(1)} %broadcast_compare_fusion.1), kind=kLoop, calls=%fused_computation.26 | loop fusion | flops 20971008 | bytes 17305600 | tf_op jit(solution)/shard_map/cond/branch_1_fun/reduce_sum | solution.py:176
  312.4 15.8 %conditional.6 = (f32[1,8,64]{2,1,0:T(8,128)S(1)}, f32[1,8,64,128]{3,2,1,0:T(8,128)S(1)}) conditional(s32[]{:T(128)} %bitcast.77, () %tuple.51, (s32[8192]{0:T(1024)S(1)}, s32[256]{0:T(256)S(1)}, bf16[8192,1,128]{2,0,1:T(8,128)(2,1)}, bf16[256,1024]{1,0:T(8,128)(2,1)}, bf16[8192,1,128]{2,0,1:T(8,128)(2,1)}) %tuple.111), branch_computations={%region_14.15_spmd, %region_15.18_spmd} | conditional | flops 2202533376 | bytes 65450796 | solution.py:189
  312.9 4.9 %fusion.40 = (f32[8,64]{1,0:T(8,128)S(1)}, f32[8192,64,8]{0,1,2:T(8,128)S(1)}) fusion(pred[64,8192]{1,0:T(8,128)(4,1)S(1)} %broadcast_compare_fusion.2, bf16[8192,1,128]{2,0,1:T(8,128)(2,1)} %get-tuple-element.107, bf16[256,1024]{1,0:T(8,128)(2,1)} %get-tuple-element.108), kind=kOutput, calls=%fused_computation.44 | convolution fusion | flops 1086324224 | bytes 19531776 | tf_op jit(solution)/shard_map/cond/branch_1_fun/bgrd,kgd->grbk/dot_general | solution.py:164
  317.8 4.8 %fusion.50 = f32[1,8,64,128]{3,2,1,0:T(8,128)S(1)} fusion(bf16[8192,1,128]{2,0,1:T(8,128)(2,1)S(1)} %copy-done.4, f32[8192,64,8]{0,1,2:T(8,128)S(1)} %get-tuple-element.183, f32[8,64]{1,0:T(8,128)S(1)} %broadcast_maximum_fusion.2, pred[64,8192]{1,0:T(8,128)(4,1)S(1)} %broadcast_compare_fusion.2), kind=kOutput, calls=%fused_computation.53 | convolution fusion | flops 1094713344 | bytes 19662848 | tf_op jit(solution)/shard_map/cond/branch_1_fun/grbk,kgd->grbd/dot_general | solution.py:177
  322.7 5.5 %fusion.42 = f32[8,64]{1,0:T(8,128)S(1)} fusion(f32[8192,64,8]{0,1,2:T(8,128)S(1)} %get-tuple-element.183, f32[8,64]{1,0:T(8,128)S(1)} %broadcast_maximum_fusion.2, pred[64,8192]{1,0:T(8,128)(4,1)S(1)} %broadcast_compare_fusion.2), kind=kLoop, calls=%fused_computation.46 | loop fusion | flops 20971008 | bytes 17305600 | tf_op jit(solution)/shard_map/cond/branch_1_fun/reduce_sum | solution.py:176
  328.1 15.5 %conditional.7 = (f32[1,8,64]{2,1,0:T(8,128)S(1)}, f32[1,8,64,128]{3,2,1,0:T(8,128)S(1)}) conditional(s32[]{:T(128)} %bitcast.78, () %tuple.52, (s32[8192]{0:T(1024)S(1)}, s32[256]{0:T(256)S(1)}, bf16[8192,1,128]{2,0,1:T(8,128)(2,1)}, bf16[256,1024]{1,0:T(8,128)(2,1)}, bf16[8192,1,128]{2,0,1:T(8,128)(2,1)}) %tuple.112), branch_computations={%region_18.19_spmd, %region_19.22_spmd} | conditional | flops 2202533376 | bytes 65450796 | solution.py:189
  328.6 4.9 %fusion.60 = (f32[8,64]{1,0:T(8,128)S(1)}, f32[8192,64,8]{0,1,2:T(8,128)S(1)}) fusion(pred[64,8192]{1,0:T(8,128)(4,1)S(1)} %broadcast_compare_fusion.3, bf16[8192,1,128]{2,0,1:T(8,128)(2,1)} %get-tuple-element.112, bf16[256,1024]{1,0:T(8,128)(2,1)} %get-tuple-element.113), kind=kOutput, calls=%fused_computation.64 | convolution fusion | flops 1086324224 | bytes 19531776 | tf_op jit(solution)/shard_map/cond/branch_1_fun/bgrd,kgd->grbk/dot_general | solution.py:164
  333.5 4.7 %fusion.70 = f32[1,8,64,128]{3,2,1,0:T(8,128)S(1)} fusion(bf16[8192,1,128]{2,0,1:T(8,128)(2,1)S(1)} %copy-done.5, f32[8192,64,8]{0,1,2:T(8,128)S(1)} %get-tuple-element.185, f32[8,64]{1,0:T(8,128)S(1)} %broadcast_maximum_fusion.3, pred[64,8192]{1,0:T(8,128)(4,1)S(1)} %broadcast_compare_fusion.3), kind=kOutput, calls=%fused_computation.73 | convolution fusion | flops 1094713344 | bytes 19662848 | tf_op jit(solution)/shard_map/cond/branch_1_fun/grbk,kgd->grbd/dot_general | solution.py:177
  338.1 5.5 %fusion.62 = f32[8,64]{1,0:T(8,128)S(1)} fusion(f32[8192,64,8]{0,1,2:T(8,128)S(1)} %get-tuple-element.185, f32[8,64]{1,0:T(8,128)S(1)} %broadcast_maximum_fusion.3, pred[64,8192]{1,0:T(8,128)(4,1)S(1)} %broadcast_compare_fusion.3), kind=kLoop, calls=%fused_computation.66 | loop fusion | flops 20971008 | bytes 17305600 | tf_op jit(solution)/shard_map/cond/branch_1_fun/reduce_sum | solution.py:176
  (79 shorter events, 19.8 us)
Async XLA Ops:
  7.2 118.8 %copy-start.1 = (f32[16]{0:T(128)S(1)}, f32[16]{0:T(128)}, u32[]{:S(2)}) copy-start(f32[16]{0:T(128)} %param.28) | copy-start | bytes 196
  7.2 119.8 %copy-start = (f32[1024]{0:T(1024)S(1)}, f32[1024]{0:T(1024)}, u32[]{:S(2)}) copy-start(f32[1024]{0:T(1024)} %param.31) | copy-start | bytes 12292
  7.2 118.7 %all-gather.10.cloned.1.call-start = ((), (), s32[]{:S(2)}) async-start(), calls=%async_computation.4 | async-start | bytes 8650752 | tf_op jit(solution)/shard_map/all_gather | solution.py:20
  8.2 16.1 %collective-permute-start = (bf16[3,1024]{0,1:T(8,128)(2,1)S(1)}, bf16[3,1024]{0,1:T(8,128)(2,1)S(1)}, u32[]{:S(2)}, u32[]{:S(2)}) collective-permute-start(bf16[3,1024]{0,1:T(8,128)(2,1)S(1)} %copy.76), channel_id=1, source_target_pairs={{0,8},{8,16},{16,24},{24,32},{32,40},{40,48},{48,56},{56,64},{64,7... | collective-permute-start | bytes 18440 | tf_op jit(solution)/shard_map/ppermute | solution.py:14
  12.7 10.1 %collective-permute-start.1 = (bf16[3,1,256]{2,0,1:T(4,128)(2,1)S(1)}, bf16[3,1,256]{2,0,1:T(4,128)(2,1)S(1)}, u32[]{:S(2)}, u32[]{:S(2)}) collective-permute-start(bf16[3,1,256]{2,0,1:T(4,128)(2,1)S(1)} %slice.125), channel_id=1, source_target_pairs={{0,8},{8,16},{16,24},{24,32},{32,40},{40,48},{48,56},{56,64},{64,7... | collective-permute-start | bytes 4616 | tf_op jit(solution)/shard_map/ppermute | solution.py:14
  26.8 176.9 %all-gather.6.cloned.1.call-start = ((), (), s32[]{:S(2)}) async-start(), calls=%async_computation.2 | async-start | bytes 2162688 | tf_op jit(solution)/shard_map/all_gather | solution.py:140
  27.5 254.0 %all-gather.8.cloned.1.call-start = ((), (), s32[]{:S(2)}) async-start(), calls=%async_computation.3 | async-start | bytes 2162688 | tf_op jit(solution)/shard_map/all_gather | solution.py:141
  28.3 317.1 %reduce-scatter.2.cloned.1.call-start = ((), (), s32[]{:S(2)}) async-start(), calls=%async_computation.1 | async-start | bytes 2359296 | tf_op jit(solution)/shard_map/reduce_scatter | solution.py:127
  281.5 5.2 %copy-start.2 = (bf16[8192,1,128]{2,0,1:T(8,128)(2,1)S(1)}, bf16[8192,1,128]{2,0,1:T(8,128)(2,1)}, u32[]{:S(2)}) copy-start(bf16[8192,1,128]{2,0,1:T(8,128)(2,1)} %get-tuple-element.99) | copy-start | bytes 6291460 | tf_op jit(solution)/shard_map/cond
  296.9 5.3 %copy-start.3 = (bf16[8192,1,128]{2,0,1:T(8,128)(2,1)S(1)}, bf16[8192,1,128]{2,0,1:T(8,128)(2,1)}, u32[]{:S(2)}) copy-start(bf16[8192,1,128]{2,0,1:T(8,128)(2,1)} %get-tuple-element.104) | copy-start | bytes 6291460 | tf_op jit(solution)/shard_map/cond
  312.6 5.3 %copy-start.4 = (bf16[8192,1,128]{2,0,1:T(8,128)(2,1)S(1)}, bf16[8192,1,128]{2,0,1:T(8,128)(2,1)}, u32[]{:S(2)}) copy-start(bf16[8192,1,128]{2,0,1:T(8,128)(2,1)} %get-tuple-element.109) | copy-start | bytes 6291460 | tf_op jit(solution)/shard_map/cond
  328.1 5.3 %copy-start.5 = (bf16[8192,1,128]{2,0,1:T(8,128)(2,1)S(1)}, bf16[8192,1,128]{2,0,1:T(8,128)(2,1)}, u32[]{:S(2)}) copy-start(bf16[8192,1,128]{2,0,1:T(8,128)(2,1)} %get-tuple-element.114) | copy-start | bytes 6291460 | tf_op jit(solution)/shard_map/cond
Sparse Core Ops, SparseCore 0:
  26.9 98.9 all-gather.9
  128.5 75.1 all-gather.5
  206.3 75.1 all-gather.7
  284.5 28.6 reduce-scatter.1
where the time goes:
time: 353 us; the launch traced here: 352 us
  waiting for transfers between devices  200 us (57%)
  matrix products  48.7 us (14%)
  blocking collectives  40.3 us (11%)
  other arithmetic  31.6 us (9%)
  between operations  16.4 us (5%)
  starting transfers between devices  7.79 us (2%)
  local copies, waits for them, and re-layouts  6.81 us (2%)
    all_gather x1, waiting for transfers between devices, per_device(): value_block = lax.all_gather(values, 'ctx', axis=0, tiled=True)  77.8 us
    all_gather x1, waiting for transfers between devices, per_device(): key_block = lax.all_gather(attention_keys, 'ctx', axis=0, tiled=True)  66.5 us
    all_gather x1, waiting for transfers between devices, prefix_2(): lax.all_gather(a.astype(kind), axis)  54.2 us
    all_gather x1, blocking collectives, prefix_2(): lax.all_gather(a.astype(kind), axis)  40.3 us
    reduce_sum x4, other arithmetic, update(): new_total = jnp.sum(weights, axis=3)  21.9 us
    dot_general x4, matrix products, update(): jnp.einsum('bgrd,kgd->grbk', query_tile_block, key_head_rows, preferred_e...  19.5 us
    dot_general x4, matrix products, update(): jnp.einsum('grbk,kgd->grbd', weights.astype(jnp.bfloat16), value_head_row...  18.8 us
    ppermute x2, starting transfers between devices, passed_along(): return lax.ppermute(shard, axis, pairs)  7.64 us
  transfers between devices with their start and end apart: 6, of which 3 were waited for; matrix products, arithmetic and copies ran while one was open for 24% of the time, Pallas kernels for 0%

commit v1 on v0

--- a/solution.py
+++ b/solution.py
@@ -137,7 +137,10 @@
     query_heads = queries.reshape(tok_rows, kv_heads, shared_heads, HEAD_SIZE)
     block_rows = tok_rows // 4
     first_key = jnp.int32(0)
-    key_block = lax.all_gather(attention_keys, "ctx", axis=0, tiled=True)
+    count = lax.axis_size("ctx")
+    blocks = jnp.stack([attention_keys for _ in range(count)])
+    blocks = lax.all_to_all(blocks, "ctx", split_axis=0, concat_axis=0)
+    key_block = jnp.concatenate(blocks, axis=0)
     value_block = lax.all_gather(values, "ctx", axis=0, tiled=True)
     key_count = key_block.shape[0]
     key_head_rows = key_block.reshape(key_count, kv_heads, HEAD_SIZE)

time: 353 us -> 291 us (0.82)
  waiting for transfers between devices: 200 us -> 75.4 us
  blocking collectives: 40.3 us -> 88.9 us
  starting transfers between devices: 7.79 us -> 17.6 us
    all_gather x1 -> x0, waiting for transfers between devices: 66.5 us -> none  [per_device(): key_block = lax.all_gather(attention_keys, 'ctx', axis=0, tiled=True)]
    all_gather x1, blocking collectives: 40.3 us -> 88.9 us  [prefix_2(): lax.all_gather(a.astype(kind), axis)]
    all_gather x1, waiting for transfers between devices: 54.2 us -> 8.53 us  [prefix_2(): lax.all_gather(a.astype(kind), axis)]
    all_gather x1, waiting for transfers between devices: 77.8 us -> 66.2 us  [per_device(): value_block = lax.all_gather(values, 'ctx', axis=0, tiled=True)]
    all_to_all x0 -> x1, starting transfers between devices: none -> 9.83 us  [per_device(): blocks = lax.all_to_all(blocks, 'ctx', split_axis=0, concat_axis=0)]
  transfers between devices with their start and end apart: 6 -> 6, of which waited for: 3 -> 2; matrix products, arithmetic and copies ran while one was open for 24% -> 30% of each run, Pallas kernels for 0% -> 0%
where the time goes in v1:
time: 291 us; the launch traced here: 289 us
  blocking collectives  88.9 us (31%)
  waiting for transfers between devices  75.4 us (26%)
  matrix products  49.1 us (17%)
  other arithmetic  31.6 us (11%)
  starting transfers between devices  17.6 us (6%)
  between operations  16.4 us (6%)
  local copies, waits for them, and re-layouts  9.46 us (3%)
    all_gather x1, blocking collectives, prefix_2(): lax.all_gather(a.astype(kind), axis)  88.9 us
    all_gather x1, waiting for transfers between devices, per_device(): value_block = lax.all_gather(values, 'ctx', axis=0, tiled=True)  66.2 us
    reduce_sum x4, other arithmetic, update(): new_total = jnp.sum(weights, axis=3)  21.9 us
    dot_general x4, matrix products, update(): jnp.einsum('grbk,kgd->grbd', weights.astype(jnp.bfloat16), value_head_row...  18.9 us
    dot_general x4, matrix products, update(): jnp.einsum('bgrd,kgd->grbk', query_tile_block, key_head_rows, preferred_e...  17.2 us
    all_to_all x1, starting transfers between devices, per_device(): blocks = lax.all_to_all(blocks, 'ctx', split_axis=0, concat_axis=0)  9.83 us
    all_gather x1, waiting for transfers between devices, prefix_2(): lax.all_gather(a.astype(kind), axis)  8.53 us
    ppermute x2, starting transfers between devices, passed_along(): return lax.ppermute(shard, axis, pairs)  7.65 us
  transfers between devices with their start and end apart: 6, of which 2 were waited for; matrix products, arithmetic and copies ran while one was open for 30% of the time, Pallas kernels for 0%

profile of v1, /device:TPU:4, one launch (start us, length us, event | category | flops | bytes accessed | tf_op | source)
XLA Modules:
  0.0 288.9 jit_solution(8687275468281543021)
XLA Ops:
  7.9 3.8 %collective-permute-start.1 = (bf16[3,1,256]{2,0,1:T(4,128)(2,1)S(1)}, bf16[3,1,256]{2,0,1:T(4,128)(2,1)S(1)}, u32[]{:S(2)}, u32[]{:S(2)}) collective-permute-start(bf16[3,1,256]{2,0,1:T(4,128)(2,1)S(1)} %slice.125), channel_id=1, source_target_pairs={{0,8},{8,16},{16,24},{24,32},{32,40},{40,48},{48,56},{56,64},{64,7... | collective-permute-start | bytes 4616 | tf_op jit(solution)/shard_map/ppermute | solution.py:14
  12.7 3.8 %collective-permute-start = (bf16[3,1024]{0,1:T(8,128)(2,1)S(1)}, bf16[3,1024]{0,1:T(8,128)(2,1)S(1)}, u32[]{:S(2)}, u32[]{:S(2)}) collective-permute-start(bf16[3,1024]{0,1:T(8,128)(2,1)S(1)} %copy.76), channel_id=1, source_target_pairs={{0,8},{8,16},{16,24},{24,32},{32,40},{40,48},{48,56},{56,64},{64,7... | collective-permute-start | bytes 18440 | tf_op jit(solution)/shard_map/ppermute | solution.py:14
  27.5 2.6 stack.2
  30.2 9.8 %all-to-all-start = ((bf16[32,256,128]{2,1,0:T(8,128)(2,1)}), bf16[32,256,128]{2,1,0:T(8,128)(2,1)S(1)}, u32[]{:S(2)}, u32[]{:S(2)}) async-start(bf16[32,256,128]{2,1,0:T(8,128)(2,1)} %stack.2), calls=%async_computation.1 | async-start | bytes 4194304 | tf_op jit(solution)/shard_map/all_to_all | solution.py:142
  40.1 88.9 %all-gather = bf16[32,16,1]{1,2,0:T(2,128)(2,1)S(1)} all-gather(bf16[1,16,1]{1,2,0:T(2,128)(2,1)S(1)} %slice.213), channel_id=2, replica_groups=mesh['ctx'=32,'tp'=8] {'ctx'}, dimensions={0}, use_global_device_ids=true | all-gather | bytes 1056 | tf_op jit(solution)/shard_map/all_gather | solution.py:20
  133.3 8.5 %all-gather.7.cloned.1.call-done = bf16[512,64,128]{2,1,0:T(8,128)(2,1)} async-done(((bf16[16,64,128]{2,1,0:T(8,128)(2,1)}), bf16[512,64,128]{2,1,0:T(8,128)(2,1)}) %all-gather.7.cloned.1.call-update) | async-done | bytes 8388624 | tf_op jit(solution)/shard_map/all_gather | solution.py:20
  144.3 7.2 %convolution_convert_fusion = bf16[256,4096]{1,0:T(8,128)(2,1)} fusion(bf16[1024,4096]{1,0:T(8,128)(2,1)} %param.32, f32[256,1024]{0,1:T(8,128)S(1)} %get-tuple-element.171, f32[1024]{0:T(1024)S(1)} %copy-done.1, f32[256]{0:T(256)S(1)} %add_rsqrt_fusion), kind=kOutput, calls=%fused_computation.82 | convolution fusion | flops 2149318656 | bytes 11539456 | tf_op jit(solution)/shard_map/dot_general | solution.py:128
  154.6 66.2 %all-gather.5.cloned.1.call-done = bf16[8192,128]{1,0:T(8,128)(2,1)} async-done(((bf16[256,128]{1,0:T(8,128)(2,1)}), bf16[8192,128]{1,0:T(8,128)(2,1)}) %all-gather.5.cloned.1.call-update) | async-done | bytes 2097168 | tf_op jit(solution)/shard_map/all_gather | solution.py:144
  220.8 14.9 %conditional.7 = (f32[1,8,64]{2,1,0:T(8,128)S(1)}, f32[1,8,64,128]{3,2,1,0:T(8,128)S(1)}) conditional(s32[]{:T(128)} %bitcast.78, () %tuple.52, (s32[8192]{0:T(1024)S(1)}, s32[256]{0:T(256)S(1)}, bf16[8192,1,128]{2,0,1:T(8,128)(2,1)S(1)}, bf16[256,1024]{1,0:T(8,128)(2,1)}, bf16[8192,1,128]{2,0,1:T(8,128)(2,1)}) %tuple.107), branch_computations={%region_18.19_spmd, %region_19.22_spmd} | conditional | flops 2202533376 | bytes 65450796 | solution.py:192
  221.2 4.3 %fusion.60 = (f32[8,64]{1,0:T(8,128)S(1)}, f32[8192,64,8]{0,1,2:T(8,128)S(1)}) fusion(pred[64,8192]{1,0:T(8,128)(4,1)S(1)} %broadcast_compare_fusion.3, bf16[8192,1,128]{2,0,1:T(8,128)(2,1)S(1)} %get-tuple-element.112, bf16[256,1024]{1,0:T(8,128)(2,1)} %get-tuple-element.113), kind=kOutput, calls=%fused_computation.64 | convolution fusion | flops 1086324224 | bytes 19531776 | tf_op jit(solution)/shard_map/cond/branch_1_fun/bgrd,kgd->grbk/dot_general | solution.py:167
  225.5 4.7 %fusion.70 = f32[1,8,64,128]{3,2,1,0:T(8,128)S(1)} fusion(bf16[8192,1,128]{2,0,1:T(8,128)(2,1)S(1)} %copy-done.3, f32[8192,64,8]{0,1,2:T(8,128)S(1)} %get-tuple-element.185, f32[8,64]{1,0:T(8,128)S(1)} %broadcast_maximum_fusion.3, pred[64,8192]{1,0:T(8,128)(4,1)S(1)} %broadcast_compare_fusion.3), kind=kOutput, calls=%fused_computation.73 | convolution fusion | flops 1094713344 | bytes 19662848 | tf_op jit(solution)/shard_map/cond/branch_1_fun/grbk,kgd->grbd/dot_general | solution.py:180
  230.2 5.5 %fusion.62 = f32[8,64]{1,0:T(8,128)S(1)} fusion(f32[8192,64,8]{0,1,2:T(8,128)S(1)} %get-tuple-element.185, f32[8,64]{1,0:T(8,128)S(1)} %broadcast_maximum_fusion.3, pred[64,8192]{1,0:T(8,128)(4,1)S(1)} %broadcast_compare_fusion.3), kind=kLoop, calls=%fused_computation.66 | loop fusion | flops 20971008 | bytes 17305600 | tf_op jit(solution)/shard_map/cond/branch_1_fun/reduce_sum | solution.py:179
  235.7 14.8 %conditional.6 = (f32[1,8,64]{2,1,0:T(8,128)S(1)}, f32[1,8,64,128]{3,2,1,0:T(8,128)S(1)}) conditional(s32[]{:T(128)} %bitcast.77, () %tuple.51, (s32[8192]{0:T(1024)S(1)}, s32[256]{0:T(256)S(1)}, bf16[8192,1,128]{2,0,1:T(8,128)(2,1)S(1)}, bf16[256,1024]{1,0:T(8,128)(2,1)}, bf16[8192,1,128]{2,0,1:T(8,128)(2,1)}) %tuple.108), branch_computations={%region_14.15_spmd, %region_15.18_spmd} | conditional | flops 2202533376 | bytes 65450796 | solution.py:192
  236.1 4.3 %fusion.40 = (f32[8,64]{1,0:T(8,128)S(1)}, f32[8192,64,8]{0,1,2:T(8,128)S(1)}) fusion(pred[64,8192]{1,0:T(8,128)(4,1)S(1)} %broadcast_compare_fusion.2, bf16[8192,1,128]{2,0,1:T(8,128)(2,1)S(1)} %get-tuple-element.107, bf16[256,1024]{1,0:T(8,128)(2,1)} %get-tuple-element.108), kind=kOutput, calls=%fused_computation.44 | convolution fusion | flops 1086324224 | bytes 19531776 | tf_op jit(solution)/shard_map/cond/branch_1_fun/bgrd,kgd->grbk/dot_general | solution.py:167
  240.4 4.7 %fusion.50 = f32[1,8,64,128]{3,2,1,0:T(8,128)S(1)} fusion(bf16[8192,1,128]{2,0,1:T(8,128)(2,1)S(1)} %copy-done.4, f32[8192,64,8]{0,1,2:T(8,128)S(1)} %get-tuple-element.183, f32[8,64]{1,0:T(8,128)S(1)} %broadcast_maximum_fusion.2, pred[64,8192]{1,0:T(8,128)(4,1)S(1)} %broadcast_compare_fusion.2), kind=kOutput, calls=%fused_computation.53 | convolution fusion | flops 1094713344 | bytes 19662848 | tf_op jit(solution)/shard_map/cond/branch_1_fun/grbk,kgd->grbd/dot_general | solution.py:180
  245.1 5.5 %fusion.42 = f32[8,64]{1,0:T(8,128)S(1)} fusion(f32[8192,64,8]{0,1,2:T(8,128)S(1)} %get-tuple-element.183, f32[8,64]{1,0:T(8,128)S(1)} %broadcast_maximum_fusion.2, pred[64,8192]{1,0:T(8,128)(4,1)S(1)} %broadcast_compare_fusion.2), kind=kLoop, calls=%fused_computation.46 | loop fusion | flops 20971008 | bytes 17305600 | tf_op jit(solution)/shard_map/cond/branch_1_fun/reduce_sum | solution.py:179
  250.5 15.4 %conditional.5 = (f32[1,8,64]{2,1,0:T(8,128)S(1)}, f32[1,8,64,128]{3,2,1,0:T(8,128)S(1)}) conditional(s32[]{:T(128)} %bitcast.76, () %tuple.50, (s32[8192]{0:T(1024)S(1)}, s32[256]{0:T(256)S(1)}, bf16[8192,1,128]{2,0,1:T(8,128)(2,1)S(1)}, bf16[256,1024]{1,0:T(8,128)(2,1)}, bf16[8192,1,128]{2,0,1:T(8,128)(2,1)}) %tuple.109), branch_computations={%region_10.11_spmd, %region_11.14_spmd} | conditional | flops 2202533376 | bytes 65450796 | solution.py:192
  251.1 4.3 %fusion.20 = (f32[8,64]{1,0:T(8,128)S(1)}, f32[8192,64,8]{0,1,2:T(8,128)S(1)}) fusion(pred[64,8192]{1,0:T(8,128)(4,1)S(1)} %broadcast_compare_fusion.1, bf16[8192,1,128]{2,0,1:T(8,128)(2,1)S(1)} %get-tuple-element.102, bf16[256,1024]{1,0:T(8,128)(2,1)} %get-tuple-element.103), kind=kOutput, calls=%fused_computation.24 | convolution fusion | flops 1086324224 | bytes 19531776 | tf_op jit(solution)/shard_map/cond/branch_1_fun/bgrd,kgd->grbk/dot_general | solution.py:167
  255.5 4.9 %fusion.30 = f32[1,8,64,128]{3,2,1,0:T(8,128)S(1)} fusion(bf16[8192,1,128]{2,0,1:T(8,128)(2,1)S(1)} %copy-done.5, f32[8192,64,8]{0,1,2:T(8,128)S(1)} %get-tuple-element.181, f32[8,64]{1,0:T(8,128)S(1)} %broadcast_maximum_fusion.1, pred[64,8192]{1,0:T(8,128)(4,1)S(1)} %broadcast_compare_fusion.1), kind=kOutput, calls=%fused_computation.33 | convolution fusion | flops 1094713344 | bytes 19662848 | tf_op jit(solution)/shard_map/cond/branch_1_fun/grbk,kgd->grbd/dot_general | solution.py:180
  260.4 5.5 %fusion.22 = f32[8,64]{1,0:T(8,128)S(1)} fusion(f32[8192,64,8]{0,1,2:T(8,128)S(1)} %get-tuple-element.181, f32[8,64]{1,0:T(8,128)S(1)} %broadcast_maximum_fusion.1, pred[64,8192]{1,0:T(8,128)(4,1)S(1)} %broadcast_compare_fusion.1), kind=kLoop, calls=%fused_computation.26 | loop fusion | flops 20971008 | bytes 17305600 | tf_op jit(solution)/shard_map/cond/branch_1_fun/reduce_sum | solution.py:179
  265.9 14.8 %conditional.4 = (f32[1,8,64]{2,1,0:T(8,128)S(1)}, f32[1,8,64,128]{3,2,1,0:T(8,128)S(1)}) conditional(s32[]{:T(128)} %bitcast.73, () %tuple.48, (s32[8192]{0:T(1024)S(1)}, s32[256]{0:T(256)S(1)}, bf16[8192,1,128]{2,0,1:T(8,128)(2,1)S(1)}, bf16[256,1024]{1,0:T(8,128)(2,1)}, bf16[8192,1,128]{2,0,1:T(8,128)(2,1)}) %tuple.110), branch_computations={%region_6.7_spmd, %region_7.10_spmd} | conditional | flops 2202533376 | bytes 65450796 | solution.py:192
  266.3 4.3 %fusion = (f32[8,64]{1,0:T(8,128)S(1)}, f32[8192,64,8]{0,1,2:T(8,128)S(1)}) fusion(pred[64,8192]{1,0:T(8,128)(4,1)S(1)} %broadcast_compare_fusion, bf16[8192,1,128]{2,0,1:T(8,128)(2,1)S(1)} %get-tuple-element.97, bf16[256,1024]{1,0:T(8,128)(2,1)} %get-tuple-element.98), kind=kOutput, calls=%fused_computation.4 | convolution fusion | flops 1086324224 | bytes 19531776 | tf_op jit(solution)/shard_map/cond/branch_1_fun/bgrd,kgd->grbk/dot_general | solution.py:167
  270.6 4.7 %fusion.10 = f32[1,8,64,128]{3,2,1,0:T(8,128)S(1)} fusion(bf16[8192,1,128]{2,0,1:T(8,128)(2,1)S(1)} %copy-done.6, f32[8192,64,8]{0,1,2:T(8,128)S(1)} %get-tuple-element.179, f32[8,64]{1,0:T(8,128)S(1)} %broadcast_maximum_fusion, pred[64,8192]{1,0:T(8,128)(4,1)S(1)} %broadcast_compare_fusion), kind=kOutput, calls=%fused_computation.13 | convolution fusion | flops 1094713344 | bytes 19662848 | tf_op jit(solution)/shard_map/cond/branch_1_fun/grbk,kgd->grbd/dot_general | solution.py:180
  275.2 5.5 %fusion.2 = f32[8,64]{1,0:T(8,128)S(1)} fusion(f32[8192,64,8]{0,1,2:T(8,128)S(1)} %get-tuple-element.179, f32[8,64]{1,0:T(8,128)S(1)} %broadcast_maximum_fusion, pred[64,8192]{1,0:T(8,128)(4,1)S(1)} %broadcast_compare_fusion), kind=kLoop, calls=%fused_computation.6 | loop fusion | flops 20971008 | bytes 17305600 | tf_op jit(solution)/shard_map/cond/branch_1_fun/reduce_sum | solution.py:179
  (81 shorter events, 23.2 us)
Async XLA Ops:
  7.2 134.8 %copy-start.2 = (f32[16]{0:T(128)S(1)}, f32[16]{0:T(128)}, u32[]{:S(2)}) copy-start(f32[16]{0:T(128)} %param.28) | copy-start | bytes 196
  7.2 134.7 %all-gather.7.cloned.1.call-start = ((), (), s32[]{:S(2)}) async-start(), calls=%async_computation.4 | async-start | bytes 8650752 | tf_op jit(solution)/shard_map/all_gather | solution.py:20
  7.9 14.9 %collective-permute-start.1 = (bf16[3,1,256]{2,0,1:T(4,128)(2,1)S(1)}, bf16[3,1,256]{2,0,1:T(4,128)(2,1)S(1)}, u32[]{:S(2)}, u32[]{:S(2)}) collective-permute-start(bf16[3,1,256]{2,0,1:T(4,128)(2,1)S(1)} %slice.125), channel_id=1, source_target_pairs={{0,8},{8,16},{16,24},{24,32},{32,40},{40,48},{48,56},{56,64},{64,7... | collective-permute-start | bytes 4616 | tf_op jit(solution)/shard_map/ppermute | solution.py:14
  12.7 11.6 %collective-permute-start = (bf16[3,1024]{0,1:T(8,128)(2,1)S(1)}, bf16[3,1024]{0,1:T(8,128)(2,1)S(1)}, u32[]{:S(2)}, u32[]{:S(2)}) collective-permute-start(bf16[3,1024]{0,1:T(8,128)(2,1)S(1)} %copy.76), channel_id=1, source_target_pairs={{0,8},{8,16},{16,24},{24,32},{32,40},{40,48},{48,56},{56,64},{64,7... | collective-permute-start | bytes 18440 | tf_op jit(solution)/shard_map/ppermute | solution.py:14
  21.6 122.7 %copy-start.1 = (f32[1024]{0:T(1024)S(1)}, f32[1024]{0:T(1024)}, u32[]{:S(2)}) copy-start(f32[1024]{0:T(1024)} %param.31) | copy-start | bytes 12292
  25.8 116.1 %copy-start = (bf16[256,1024]{0,1:T(8,128)(2,1)}, bf16[256,1024]{0,1:T(8,128)(2,1)S(1)}, u32[]{:S(2)}) copy-start(bf16[256,1024]{0,1:T(8,128)(2,1)S(1)} %get-tuple-element.175) | copy-start | bytes 1572868
  26.8 194.0 %all-gather.5.cloned.1.call-start = ((), (), s32[]{:S(2)}) async-start(), calls=%async_computation.3 | async-start | bytes 2162688 | tf_op jit(solution)/shard_map/all_gather | solution.py:144
  30.2 190.6 %all-to-all-start = ((bf16[32,256,128]{2,1,0:T(8,128)(2,1)}), bf16[32,256,128]{2,1,0:T(8,128)(2,1)S(1)}, u32[]{:S(2)}, u32[]{:S(2)}) async-start(bf16[32,256,128]{2,1,0:T(8,128)(2,1)} %stack.2), calls=%async_computation.1 | async-start | bytes 4194304 | tf_op jit(solution)/shard_map/all_to_all | solution.py:142
  40.0 242.4 %reduce-scatter.2.cloned.1.call-start = ((), (), s32[]{:S(2)}) async-start(), calls=%async_computation.2 | async-start | bytes 2359296 | tf_op jit(solution)/shard_map/reduce_scatter | solution.py:127
  220.8 4.7 %copy-start.3 = (bf16[8192,1,128]{2,0,1:T(8,128)(2,1)S(1)}, bf16[8192,1,128]{2,0,1:T(8,128)(2,1)}, u32[]{:S(2)}) copy-start(bf16[8192,1,128]{2,0,1:T(8,128)(2,1)} %get-tuple-element.114) | copy-start | bytes 6291460 | tf_op jit(solution)/shard_map/cond
  235.7 4.7 %copy-start.4 = (bf16[8192,1,128]{2,0,1:T(8,128)(2,1)S(1)}, bf16[8192,1,128]{2,0,1:T(8,128)(2,1)}, u32[]{:S(2)}) copy-start(bf16[8192,1,128]{2,0,1:T(8,128)(2,1)} %get-tuple-element.109) | copy-start | bytes 6291460 | tf_op jit(solution)/shard_map/cond
  250.7 4.8 %copy-start.5 = (bf16[8192,1,128]{2,0,1:T(8,128)(2,1)S(1)}, bf16[8192,1,128]{2,0,1:T(8,128)(2,1)}, u32[]{:S(2)}) copy-start(bf16[8192,1,128]{2,0,1:T(8,128)(2,1)} %get-tuple-element.104) | copy-start | bytes 6291460 | tf_op jit(solution)/shard_map/cond
  265.9 4.7 %copy-start.6 = (bf16[8192,1,128]{2,0,1:T(8,128)(2,1)S(1)}, bf16[8192,1,128]{2,0,1:T(8,128)(2,1)}, u32[]{:S(2)}) copy-start(bf16[8192,1,128]{2,0,1:T(8,128)(2,1)} %get-tuple-element.99) | copy-start | bytes 6291460 | tf_op jit(solution)/shard_map/cond
Sparse Core Ops, SparseCore 0:
  26.9 114.8 all-gather.6
  144.4 76.2 all-gather.4
  223.9 28.5 reduce-scatter.1
